TPU v7x, 512 devices: a whole 4x4x16 slice. The times are simulated.
512 devices in a mesh: narrow: 16 (over z), wide: 32 (over y, x, core).
Axes of the slice: x: 4, y: 4, z: 16, core: 2. Of those that a mesh axis runs over, the one named last changes fastest.
Arguments:
- sources: float32 [16, 64, 128, 256], P(None, 'wide', 'narrow')
- well_columns: int32 [16], replicated, may hold values from 0 to 8191
- column_active: int32 [64, 128], P('wide', 'narrow'), may hold values 0 or 1
- perm_root: float32 [64, 128, 256], P('wide', 'narrow'), may hold values from 0.5 to 2
- storage_term: float32 [64, 128, 256], P('wide', 'narrow'), may hold values from 0.2 to 2
- inverse_blocks: bfloat16 [64, 128, 2, 128, 128], P('wide', 'narrow')
Outputs:
- solution: float32 [16, 64, 128, 256], P(None, 'wide', 'narrow')
- residual: float32 [16, 64, 128, 256], P(None, 'wide', 'narrow')
All inputs are finite; a program needn't handle non-finite values. No bound on the sum of `column_active` on one device may be relied on, other than what follows from the above.
Results may differ from a plain program's by a relative error of at most 0.0085.
Values sent between devices are 32-bit elements; how exact they have to be, the bound alone decides.
A program may use at most 64 MiB of HBM per device.

v0:
```python
import jax
import jax.numpy as jnp
from jax import lax
from jax.sharding import PartitionSpec as P

ITERS = 3
WELL_RATE = 4.0


def with_halo(x, sides, width):
    for axis, dim in sides:
        peers, length = (lax.axis_size(axis), x.shape[dim])
        up = [(i, (i + 1) % peers) for i in range(peers - 1)]
        down = [(j, i) for i, j in up]
        last = lax.slice_in_dim(x, length - width, length, axis=dim)
        first = lax.slice_in_dim(x, 0, width, axis=dim)
        before = lax.ppermute(last, axis, up)
        after = lax.ppermute(first, axis, down)
        x = jnp.concatenate([before, x, after], axis=dim)
    return x


def coupling(padded, coef_pad):
    center = padded[:, 1:-1, 1:-1]
    coef = coef_pad[1:-1, 1:-1]
    total = coef_pad[2:, 1:-1] * (center - padded[:, 2:, 1:-1]) + coef_pad[:-2, 1:-1] * (
        center - padded[:, :-2, 1:-1]
    )
    total = (
        total
        + coef_pad[1:-1, 2:] * (center - padded[:, 1:-1, 2:])
        + coef_pad[1:-1, :-2] * (center - padded[:, 1:-1, :-2])
    )
    zero_layer = jnp.zeros_like(center[..., :1])
    zero_coef = jnp.zeros_like(coef[..., :1])
    upper = jnp.concatenate([center[..., 1:], zero_layer], -1)
    upper_coef = jnp.concatenate([coef[..., 1:], zero_coef], -1)
    lower = jnp.concatenate([zero_layer, center[..., :-1]], -1)
    lower_coef = jnp.concatenate([zero_coef, coef[..., :-1]], -1)
    total = total + upper_coef * (center - upper) + lower_coef * (center - lower)
    return coef * total


def operate(values, diag_term, coef, coef_pad):
    if coef_pad is None:
        stacked = jnp.concatenate([values, coef[None]], 0)
    else:
        stacked = values
    padded = with_halo(stacked, (("narrow", 2), ("wide", 1)), 1)
    if coef_pad is None:
        coef_pad = padded[-1]
        padded = padded[:-1]
    return (diag_term * values + coupling(padded, coef_pad), coef_pad)


def precondition(values, inverse_blocks):
    count, cols_x, cols_y, layers = values.shape
    blocks = inverse_blocks.shape[2]
    shaped = values.astype(jnp.bfloat16).reshape(count, cols_x, cols_y, blocks, layers // blocks)
    output = jnp.einsum(
        "xybij,kxybj->kxybi", inverse_blocks, shaped, preferred_element_type=jnp.float32
    )
    return output.reshape(count, cols_x, cols_y, layers)


def local_gram(left, right):
    return jnp.einsum("kxyz,lxyz->kl", left, right, precision=lax.Precision.HIGHEST)


def combine(values, coefs):
    return jnp.einsum("kxyz,kl->lxyz", values, coefs, precision=lax.Precision.HIGHEST)


def solve_gram(matrix, target):
    sym = 0.5 * (matrix + matrix.T)
    factor = jnp.linalg.cholesky(sym)
    inner = lax.linalg.triangular_solve(factor, target, left_side=True, lower=True)
    return lax.linalg.triangular_solve(factor, inner, left_side=True, lower=True, transpose_a=True)


def residual_sum(left, right):
    return lax.psum(local_gram(left, right), ("narrow", "wide"))


def curvature_sum(left, right):
    return lax.psum(local_gram(left, right), ("narrow", "wide"))


def on_device(sources, well_columns, column_active, perm_root, storage_term, inverse_blocks):
    cols_x, cols_y = column_active.shape
    grid_y = cols_y * lax.axis_size("narrow")
    first_x = lax.axis_index("wide") * cols_x
    first_y = lax.axis_index("narrow") * cols_y
    column_ids = (
        (first_x + jnp.arange(cols_x, dtype=jnp.int32))[:, None] * grid_y
        + first_y
        + jnp.arange(cols_y, dtype=jnp.int32)[None, :]
    )
    wells = (column_ids[None] == well_columns[:, None, None]).astype(jnp.float32)
    active = column_active.astype(jnp.float32)[..., None]
    coef = perm_root * active
    diag_term = active * storage_term + (1.0 - active)
    residual = sources + WELL_RATE * wells[..., None]
    solution = jnp.zeros_like(residual)
    zset = precondition(residual, inverse_blocks)
    coef_pad = None
    res_gram = residual_sum(zset, residual)
    direction = zset
    for iteration in range(ITERS):
        image, coef_pad = operate(direction, diag_term, coef, coef_pad)
        curv_gram = curvature_sum(direction, image)
        step_size = solve_gram(curv_gram, res_gram)
        solution = solution + combine(direction, step_size)
        residual = residual - combine(image, step_size)
        if iteration + 1 < ITERS:
            zset = precondition(residual, inverse_blocks)
            new_gram = residual_sum(zset, residual)
            conj_coef = solve_gram(res_gram, new_gram)
            direction = zset + combine(direction, conj_coef)
            res_gram = new_gram
    return (solution, residual)


def solution(mesh):
    in_specs = (
        P(None, "wide", "narrow", None),
        P(),
        P("wide", "narrow"),
        P("wide", "narrow", None),
        P("wide", "narrow", None),
        P("wide", "narrow", None, None, None),
    )
    out_specs = (P(None, "wide", "narrow", None), P(None, "wide", "narrow", None))
    return jax.shard_map(
        on_device, mesh=mesh, in_specs=in_specs, out_specs=out_specs, check_vma=False
    )
```

profile of v0, /device:TPU:1, one launch (start us, length us, event | category | flops | bytes accessed | tf_op | source)
XLA Modules:
  0.0 604.0 jit_solution(7045459315750668547)
XLA Ops:
  0.7 0.7 copy-done.3
  1.5 0.8 multiply_add_fusion
  3.0 1.6 convolution_bitcast_fusion.2
  5.1 1.3 collective-permute-start.1
  6.4 5.0 collective-permute-start
  11.4 1.1 collective-permute-done
  12.6 8.9 %collective-permute-start.3 = (f32[17,1,10,256]{3,0,2,1:T(8,128)S(1)}, f32[17,1,10,256]{3,0,2,1:T(8,128)S(1)}, u32[]{:S(2)}, u32[]{:S(2)}) collective-permute-start(f32[17,1,10,256]{3,0,2,1:T(8,128)S(1)} %get-tuple-element.11), channel_id=1, source_target_pairs={{1,0},{2,1},{3,2},{4,3},{5,4},{6,5},{7,6},{8,7},{9,8},{10,9},{11,1... | collective-permute-start | bytes 522248 | tf_op jit(solution)/shard_map/ppermute | solution.py:18
  21.5 1.9 collective-permute-start.2
  23.9 0.8 copy-done.1
  24.7 0.7 convolution_bitcast_fusion.12
  25.4 1.1 collective-permute-done.2
  27.7 109.5 %all-reduce.8 = (f32[16,16]{1,0:T(8,128)S(1)}, f32[16,16]{1,0:T(8,128)S(1)}) all-reduce(f32[16,16]{1,0:T(8,128)S(1)} %convolution_bitcast_fusion.12, f32[16,16]{1,0:T(8,128)S(1)} %convolution_bitcast_fusion.13), channel_id=1, replica_groups=mesh['narrow'=16,'wide'=32] {'narrow','wide'}, use_global_device_ids=true, to_apply=%region_3.0 | all-reduce | flops 512 | bytes 4096 | tf_op jit(solution)/shard_map/psum | solution.py:82
  137.5 1.5 cholesky.100
  138.9 0.6 compare_reduce_fusion.3
  139.6 0.6 fusion.58
  140.3 1.2 custom-call.19
  141.6 1.5 cholesky.89
  143.1 0.6 compare_reduce_fusion.4
  143.7 0.6 fusion.57
  144.4 1.2 custom-call.17
  147.8 100.5 %psum.44 = f32[16,16]{1,0:T(8,128)S(1)} all-reduce(f32[16,16]{1,0:T(8,128)S(1)} %convolution_bitcast_fusion.11), channel_id=1, replica_groups=mesh['narrow'=16,'wide'=32] {'narrow','wide'}, use_global_device_ids=true, to_apply=%region_4.8 | all-reduce | flops 256 | bytes 2048 | tf_op jit(solution)/shard_map/psum | solution.py:82
  249.6 1.5 cholesky.122
  251.1 0.6 compare_reduce_fusion.1
  251.7 1.3 collective-permute-start.5
  253.0 4.0 collective-permute-start.4
  257.0 0.7 fusion.60
  257.7 1.2 custom-call.23
  259.0 3.1 collective-permute-start.6
  262.1 2.4 collective-permute-start.7
  265.6 1.2 collective-permute-done.7
  267.5 103.6 %psum.45 = f32[16,16]{1,0:T(8,128)S(1)} all-reduce(f32[16,16]{1,0:T(8,128)S(1)} %convolution_bitcast_fusion.10), channel_id=1, replica_groups=mesh['narrow'=16,'wide'=32] {'narrow','wide'}, use_global_device_ids=true, to_apply=%region_5.9 | all-reduce | flops 256 | bytes 2048 | tf_op jit(solution)/shard_map/psum | solution.py:86
  371.3 1.5 cholesky.111
  372.7 0.6 compare_reduce_fusion.2
  373.4 0.6 fusion.59
  374.1 1.2 custom-call.21
  377.2 100.1 %psum.46 = f32[16,16]{1,0:T(8,128)S(1)} all-reduce(f32[16,16]{1,0:T(8,128)S(1)} %convolution_bitcast_fusion.9), channel_id=1, replica_groups=mesh['narrow'=16,'wide'=32] {'narrow','wide'}, use_global_device_ids=true, to_apply=%region_6.10 | all-reduce | flops 256 | bytes 2048 | tf_op jit(solution)/shard_map/psum | solution.py:82
  478.1 1.3 collective-permute-start.9
  479.4 4.0 collective-permute-start.8
  484.4 3.7 collective-permute-start.10
  488.2 2.1 collective-permute-start.11
  490.4 0.9 collective-permute-done.10
  491.4 1.2 collective-permute-done.11
  493.2 103.8 %psum.47 = f32[16,16]{1,0:T(8,128)S(1)} all-reduce(f32[16,16]{1,0:T(8,128)S(1)} %convolution_bitcast_fusion.8), channel_id=1, replica_groups=mesh['narrow'=16,'wide'=32] {'narrow','wide'}, use_global_device_ids=true, to_apply=%region_7.11 | all-reduce | flops 256 | bytes 2048 | tf_op jit(solution)/shard_map/psum | solution.py:86
  597.2 1.5 cholesky.133
  599.3 0.6 fusion.61
  600.0 1.2 custom-call.25
  602.3 0.9 copy.78
  603.2 0.9 copy.79
  (105 shorter events, 15.2 us)
Async XLA Ops:
  0.6 2.4 copy-start
  0.6 0.8 copy-start.3
  0.7 0.8 copy-start.2
  2.3 0.7 copy-start.4
  5.1 6.3 %collective-permute-start.1 = (f32[17,2,1,256]{3,0,2,1:T(8,128)S(1)}, f32[17,2,1,256]{3,0,2,1:T(8,128)S(1)}, u32[]{:S(2)}, u32[]{:S(2)}) collective-permute-start(f32[17,2,1,256]{3,0,2,1:T(8,128)S(1)} %get-tuple-element.13), channel_id=1, source_target_pairs={{32,0},{64,32},{96,64},{128,96},{160,128},{192,160},{224,192},{256... | collective-permute-start | bytes 104456 | tf_op jit(solution)/shard_map/ppermute | solution.py:18
  6.4 6.2 %collective-permute-start = (f32[17,2,1,256]{3,0,2,1:T(8,128)S(1)}, f32[17,2,1,256]{3,0,2,1:T(8,128)S(1)}, u32[]{:S(2)}, u32[]{:S(2)}) collective-permute-start(f32[17,2,1,256]{3,0,2,1:T(8,128)S(1)} %get-tuple-element.14), channel_id=1, source_target_pairs={{0,32},{32,64},{64,96},{96,128},{128,160},{160,192},{192,224},{224... | collective-permute-start | bytes 104456 | tf_op jit(solution)/shard_map/ppermute | solution.py:17
  12.6 12.8 %collective-permute-start.3 = (f32[17,1,10,256]{3,0,2,1:T(8,128)S(1)}, f32[17,1,10,256]{3,0,2,1:T(8,128)S(1)}, u32[]{:S(2)}, u32[]{:S(2)}) collective-permute-start(f32[17,1,10,256]{3,0,2,1:T(8,128)S(1)} %get-tuple-element.11), channel_id=1, source_target_pairs={{1,0},{2,1},{3,2},{4,3},{5,4},{6,5},{7,6},{8,7},{9,8},{10,9},{11,1... | collective-permute-start | bytes 522248 | tf_op jit(solution)/shard_map/ppermute | solution.py:18
  21.5 5.0 collective-permute-start.2
  23.8 1.0 copy-start.1
  251.7 7.2 %collective-permute-start.5 = (f32[16,2,1,256]{3,0,2,1:T(8,128)S(1)}, f32[16,2,1,256]{3,0,2,1:T(8,128)S(1)}, u32[]{:S(2)}, u32[]{:S(2)}) collective-permute-start(f32[16,2,1,256]{3,0,2,1:T(8,128)S(1)} %get-tuple-element.25), channel_id=1, source_target_pairs={{32,0},{64,32},{96,64},{128,96},{160,128},{192,160},{224,192},{256... | collective-permute-start | bytes 98312 | tf_op jit(solution)/shard_map/ppermute | solution.py:18
  253.0 5.9 collective-permute-start.4
  259.0 6.6 %collective-permute-start.6 = (f32[16,1,10,256]{3,0,2,1:T(8,128)S(1)}, f32[16,1,10,256]{3,0,2,1:T(8,128)S(1)}, u32[]{:S(2)}, u32[]{:S(2)}) collective-permute-start(f32[16,1,10,256]{3,0,2,1:T(8,128)S(1)} %get-tuple-element.17), channel_id=1, source_target_pairs={{1,0},{2,1},{3,2},{4,3},{5,4},{6,5},{7,6},{8,7},{9,8},{10,9},{11,1... | collective-permute-start | bytes 491528 | tf_op jit(solution)/shard_map/ppermute | solution.py:18
  262.1 4.7 collective-permute-start.7
  478.1 5.7 collective-permute-start.9
  479.4 5.0 collective-permute-start.8
  484.4 6.9 %collective-permute-start.10 = (f32[16,1,10,256]{3,0,2,1:T(8,128)S(1)}, f32[16,1,10,256]{3,0,2,1:T(8,128)S(1)}, u32[]{:S(2)}, u32[]{:S(2)}) collective-permute-start(f32[16,1,10,256]{3,0,2,1:T(8,128)S(1)} %get-tuple-element.15), channel_id=1, source_target_pairs={{1,0},{2,1},{3,2},{4,3},{5,4},{6,5},{7,6},{8,7},{9,8},{10,9},{11,1... | collective-permute-start | bytes 491528 | tf_op jit(solution)/shard_map/ppermute | solution.py:18
  488.2 4.4 collective-permute-start.11
where the time goes:
time: 605 us; the launch traced here: 604 us
  blocking collectives  517 us (85%)
  starting transfers between devices  39.1 us (6%)
  other arithmetic  22 us (4%)
  matrix products  11.4 us (2%)
  waiting for transfers between devices  6.8 us (1%)
  local copies, waits for them, and re-layouts  6.24 us (1%)
    psum x3, blocking collectives, residual_sum(): return lax.psum(local_gram(left, right), ('narrow', 'wide'))  310 us
    psum x2, blocking collectives, curvature_sum(): return lax.psum(local_gram(left, right), ('narrow', 'wide'))  207 us
    ppermute x6, starting transfers between devices, with_halo(): after = lax.ppermute(first, axis, down)  19.6 us
    ppermute x6, starting transfers between devices, with_halo(): before = lax.ppermute(last, axis, up)  19.5 us
  transfers between devices with their start and end apart: 12, of which 7 were waited for; matrix products, arithmetic and copies ran while one was open for 1% of the time, Pallas kernels for 0%

commit v1 on v0

--- a/solution.py
+++ b/solution.py
@@ -79,7 +79,7 @@
 
 
 def residual_sum(left, right):
-    return lax.psum(local_gram(left, right), ("narrow", "wide"))
+    return jnp.sum(lax.all_gather(local_gram(left, right), ("narrow", "wide")), axis=0)
 
 
 def curvature_sum(left, right):

time: 605 us -> 843 us (1.39)
  blocking collectives: 517 us -> 752 us
  other arithmetic: 22 us -> 32.6 us
    all_gather x0 -> x3, blocking collectives: none -> 438 us  [residual_sum(): lax.all_gather(local_gram(left, right), ('narrow', 'wide'))]
    psum x3 -> x0, blocking collectives: 310 us -> none  [residual_sum(): return lax.psum(local_gram(left, right), ('narrow', 'wide'))]
    psum x2 -> x3, blocking collectives: 207 us -> 313 us  [curvature_sum(): return lax.psum(local_gram(left, right), ('narrow', 'wide'))]
where the time goes in v1:
time: 843 us; the launch traced here: 842 us
  blocking collectives  752 us (89%)
  starting transfers between devices  33.8 us (4%)
  other arithmetic  32.6 us (4%)
  matrix products  12.3 us (1%)
    all_gather x3, blocking collectives, residual_sum(): lax.all_gather(local_gram(left, right), ('narrow', 'wide'))  438 us
    psum x3, blocking collectives, curvature_sum(): return lax.psum(local_gram(left, right), ('narrow', 'wide'))  313 us
    ppermute x6, starting transfers between devices, with_halo(): before = lax.ppermute(last, axis, up)  22.1 us
  transfers between devices with their start and end apart: 12, of which 7 were waited for; matrix products, arithmetic and copies ran while one was open for 1% of the time, Pallas kernels for 0%

profile of v1, /device:TPU:1, one launch (start us, length us, event | category | flops | bytes accessed | tf_op | source)
XLA Modules:
  0.0 842.0 jit_solution(4701814538702230624)
XLA Ops:
  0.6 0.8 broadcast_subtract_fusion
  1.4 0.7 convert_element_type.15
  2.2 0.8 multiply_add_fusion
  3.0 0.7 compare_select_fusion
  3.7 1.6 convolution_bitcast_fusion.2
  5.8 1.3 collective-permute-start.1
  7.1 5.0 collective-permute-start
  12.1 1.7 convolution_bitcast_fusion.12
  13.9 152.7 %all-gather = f32[8192,16]{1,0:T(8,128)} all-gather(f32[16,16]{1,0:T(8,128)S(1)} %convolution_bitcast_fusion.12), channel_id=2, replica_groups=mesh['narrow'=16,'wide'=32] {'narrow','wide'}, dimensions={0}, use_global_device_ids=true | all-gather | bytes 525312 | tf_op jit(solution)/shard_map/all_gather | solution.py:82
  166.6 2.7 reduce_sum.27
  169.5 1.5 cholesky.100
  172.1 0.7 fusion.92
  172.8 2.1 collective-permute-start.3
  174.8 3.5 collective-permute-start.2
  179.0 1.2 custom-call.19
  180.5 1.0 collective-permute-done.2
  182.7 105.1 %psum.21 = f32[16,16]{1,0:T(8,128)S(1)} all-reduce(f32[16,16]{1,0:T(8,128)S(1)} %convolution_bitcast_fusion.13), channel_id=1, replica_groups=mesh['narrow'=16,'wide'=32] {'narrow','wide'}, use_global_device_ids=true, to_apply=%region_0.0 | all-reduce | flops 256 | bytes 2048 | tf_op jit(solution)/shard_map/psum | solution.py:86
  288.0 1.5 cholesky.89
  289.4 0.7 compare_reduce_fusion.4
  290.2 0.7 fusion.57
  290.9 1.2 custom-call.17
  294.3 142.8 %all-gather.1 = f32[8192,16]{1,0:T(8,128)} all-gather(f32[16,16]{1,0:T(8,128)S(1)} %convolution_bitcast_fusion.11), channel_id=3, replica_groups=mesh['narrow'=16,'wide'=32] {'narrow','wide'}, dimensions={0}, use_global_device_ids=true | all-gather | bytes 525312 | tf_op jit(solution)/shard_map/all_gather | solution.py:82
  437.2 2.8 reduce_sum.28
  441.2 1.5 cholesky.122
  442.7 0.7 compare_reduce_fusion.1
  443.4 1.3 collective-permute-start.5
  444.7 4.0 collective-permute-start.4
  448.7 0.7 fusion.60
  449.4 1.2 custom-call.23
  450.7 2.6 collective-permute-start.6
  453.3 3.0 collective-permute-start.7
  457.4 1.2 collective-permute-done.7
  459.3 104.1 %psum.22 = f32[16,16]{1,0:T(8,128)S(1)} all-reduce(f32[16,16]{1,0:T(8,128)S(1)} %convolution_bitcast_fusion.10), channel_id=1, replica_groups=mesh['narrow'=16,'wide'=32] {'narrow','wide'}, use_global_device_ids=true, to_apply=%region_5.9 | all-reduce | flops 256 | bytes 2048 | tf_op jit(solution)/shard_map/psum | solution.py:86
  563.5 1.5 cholesky.111
  566.3 1.2 custom-call.21
  569.4 142.6 %all-gather.2 = f32[8192,16]{1,0:T(8,128)} all-gather(f32[16,16]{1,0:T(8,128)S(1)} %convolution_bitcast_fusion.9), channel_id=4, replica_groups=mesh['narrow'=16,'wide'=32] {'narrow','wide'}, dimensions={0}, use_global_device_ids=true | all-gather | bytes 525312 | tf_op jit(solution)/shard_map/all_gather | solution.py:82
  712.0 2.7 reduce_sum.29
  715.5 1.3 collective-permute-start.9
  716.8 4.0 collective-permute-start.8
  721.9 3.2 collective-permute-start.10
  725.1 2.7 collective-permute-start.11
  727.9 0.9 collective-permute-done.10
  728.8 1.2 collective-permute-done.11
  730.7 104.3 %psum.23 = f32[16,16]{1,0:T(8,128)S(1)} all-reduce(f32[16,16]{1,0:T(8,128)S(1)} %convolution_bitcast_fusion.8), channel_id=1, replica_groups=mesh['narrow'=16,'wide'=32] {'narrow','wide'}, use_global_device_ids=true, to_apply=%region_7.11 | all-reduce | flops 256 | bytes 2048 | tf_op jit(solution)/shard_map/psum | solution.py:86
  835.1 1.5 cholesky.133
  837.9 1.2 custom-call.25
  840.3 0.9 copy.78
  841.1 0.9 copy.79
  (112 shorter events, 18.0 us)
Async XLA Ops:
  0.6 3.1 copy-start
  5.8 166.2 %collective-permute-start.1 = (f32[17,2,1,256]{3,0,2,1:T(8,128)S(1)}, f32[17,2,1,256]{3,0,2,1:T(8,128)S(1)}, u32[]{:S(2)}, u32[]{:S(2)}) collective-permute-start(f32[17,2,1,256]{3,0,2,1:T(8,128)S(1)} %get-tuple-element.11), channel_id=1, source_target_pairs={{32,0},{64,32},{96,64},{128,96},{160,128},{192,160},{224,192},{256... | collective-permute-start | bytes 104456 | tf_op jit(solution)/shard_map/ppermute | solution.py:18
  7.1 164.9 %collective-permute-start = (f32[17,2,1,256]{3,0,2,1:T(8,128)S(1)}, f32[17,2,1,256]{3,0,2,1:T(8,128)S(1)}, u32[]{:S(2)}, u32[]{:S(2)}) collective-permute-start(f32[17,2,1,256]{3,0,2,1:T(8,128)S(1)} %get-tuple-element.12), channel_id=1, source_target_pairs={{0,32},{32,64},{64,96},{96,128},{128,160},{160,192},{192,224},{224... | collective-permute-start | bytes 104456 | tf_op jit(solution)/shard_map/ppermute | solution.py:17
  169.4 123.2 %copy-start.1 = (f32[16,2,8,256]{3,2,1,0:T(8,128)S(1)}, f32[16,2,8,256]{3,2,1,0:T(8,128)}, u32[]{:S(2)}) copy-start(f32[16,2,8,256]{3,2,1,0:T(8,128)} %param.11) | copy-start | bytes 786436
  172.8 7.7 collective-permute-start.3
  174.8 6.6 collective-permute-start.2
  181.8 110.5 %copy-start.2 = (f32[2,8,256]{2,1,0:T(8,128)}, f32[2,8,256]{2,1,0:T(8,128)S(1)}, u32[]{:S(2)}) copy-start(f32[2,8,256]{2,1,0:T(8,128)S(1)} %copy.40) | copy-start | bytes 49156
  181.8 110.5 %copy-start.4 = (f32[2,8,256]{2,1,0:T(8,128)}, f32[2,8,256]{2,1,0:T(8,128)S(1)}, u32[]{:S(2)}) copy-start(f32[2,8,256]{2,1,0:T(8,128)S(1)} %copy.38) | copy-start | bytes 49156
  437.2 21.4 %copy-start.3 = (f32[2,8,256]{2,1,0:T(8,128)S(1)}, f32[2,8,256]{2,1,0:T(8,128)}, u32[]{:S(2)}) copy-start(f32[2,8,256]{2,1,0:T(8,128)} %copy-done.2) | copy-start | bytes 49156
  437.2 21.4 %copy-start.5 = (f32[2,8,256]{2,1,0:T(8,128)S(1)}, f32[2,8,256]{2,1,0:T(8,128)}, u32[]{:S(2)}) copy-start(f32[2,8,256]{2,1,0:T(8,128)} %copy-done.4) | copy-start | bytes 49156
  443.4 7.2 collective-permute-start.5
  444.7 5.9 collective-permute-start.4
  450.7 6.6 collective-permute-start.6
  453.3 5.2 collective-permute-start.7
  715.5 5.7 collective-permute-start.9
  716.8 5.0 collective-permute-start.8
  721.9 6.9 collective-permute-start.10
  725.1 4.9 collective-permute-start.11
